TPU v7x, 256 devices: a whole 4x4x8 slice. The times are simulated.
256 devices in a mesh: gx: 32 (over x_hi, z, core), gy: 8 (over y, x_lo).
Axes of the slice: x: 4 (x_hi: 2, x_lo: 2; x = x_hi * 2 + x_lo), y: 4, z: 8, core: 2. Of those that a mesh axis runs over, the one named last changes fastest.
Arguments:
- adjoint_out: bfloat16 [1024, 4096, 128], P('gx', 'gy'), may hold values from -6 to 6
- shift_x: int32 [128], replicated, may hold values from -8 to 8, as said below
- shift_y: int32 [128], replicated, may hold values from -8 to 8, as said below
- frac_x: float32 [128], replicated, may hold values from 0 to 1
- frac_y: float32 [128], replicated, may hold values from 0 to 1
Outputs:
- adjoint_in: float32 [1024, 4096, 128], P('gx', 'gy')
Inputs may be any that keep to these rules, and one draw needn't show every extreme that they name: `shift_x`: signed cell shift of each velocity along x; both 8 and -8 occur. `shift_y`: signed cell shift of each velocity along y; both 8 and -8 occur.
All inputs are finite; a program needn't handle non-finite values.
Results may differ from a plain program's by a relative error of at most 0.0003.
Values may be sent and summed in bfloat16 or wider, within the bound.
A program may use at most 64 MiB of HBM per device.

v0:
```python
import jax
import jax.numpy as jnp
from jax import lax
from jax.sharding import PartitionSpec as P

REACH = 8


def with_halo(cells, sides, width):
    for axis, dim in sides:
        count = lax.axis_size(axis)
        head = lax.slice_in_dim(cells, 0, width, axis=dim)
        tail = lax.slice_in_dim(cells, cells.shape[dim] - width, cells.shape[dim], axis=dim)
        cells = jnp.concatenate(
            [
                lax.ppermute(tail, axis, [(i, (i + 1) % count) for i in range(count)]),
                cells,
                lax.ppermute(head, axis, [((i + 1) % count, i) for i in range(count)]),
            ],
            axis=dim,
        )
    return cells


def coef_table(shift, frac):
    weights = jnp.stack(
        [
            -frac * (frac - 1.0) * (frac - 2.0) / 6.0,
            (frac + 1.0) * (frac - 1.0) * (frac - 2.0) / 2.0,
            -(frac + 1.0) * frac * (frac - 2.0) / 2.0,
            (frac + 1.0) * frac * (frac - 1.0) / 6.0,
        ]
    )
    offsets = jnp.arange(2 * REACH + 4, dtype=jnp.int32) - (REACH + 2)
    taps = jnp.arange(4, dtype=jnp.int32)
    hits = shift[None, None, :] - taps[None, :, None] + 1 == offsets[:, None, None]
    return jnp.sum(
        jnp.where(hits, weights[None, :, :], jnp.zeros_like(weights[None, :, :])), axis=1
    )


def sweep(padded, coef, axis_dim, count):
    shape = list(padded.shape)
    shape[axis_dim] = count
    total = jnp.zeros(tuple(shape), jnp.float32)
    for index in range(2 * REACH + 4):
        piece = lax.slice_in_dim(padded, index, index + count, axis=axis_dim)
        total = total + coef[index][None, None, :] * piece.astype(jnp.float32)
    return total


def body(adjoint_out, shift_x, shift_y, frac_x, frac_y):
    coef_x = coef_table(shift_x, frac_x)
    coef_y = coef_table(shift_y, frac_y)
    rows_x = adjoint_out.shape[0]
    rows_y = adjoint_out.shape[1]
    padded_y = with_halo(adjoint_out, (("gy", 1),), REACH + 2)
    middle = sweep(padded_y, coef_y, 1, rows_y)
    padded_x = with_halo(middle, (("gx", 0),), REACH + 2)
    result = sweep(padded_x, coef_x, 0, rows_x)
    return result


def solution(mesh):
    return jax.shard_map(
        body,
        mesh=mesh,
        in_specs=(P("gx", "gy", None), P(), P(), P(), P()),
        out_specs=P("gx", "gy", None),
        check_vma=False,
    )
```

profile of v0, /device:TPU:26, one launch (start us, length us, event | category | flops | bytes accessed | tf_op | source)
XLA Modules:
  0.0 140.2 jit_solution(7798135273131210196)
XLA Ops:
  0.0 1.0 fusion.65
  1.0 0.6 collective-permute-start.1
  1.6 3.6 %collective-permute-start = (bf16[32,10,128]{2,1,0:T(8,128)(2,1)S(1)}, bf16[32,10,128]{2,1,0:T(8,128)(2,1)S(1)}, u32[]{:S(2)}, u32[]{:S(2)}) collective-permute-start(bf16[32,10,128]{2,1,0:T(8,128)(2,1)S(1)} %get-tuple-element.10), channel_id=1, source_target_pairs={{0,1},{1,2},{2,3},{3,4},{4,5},{5,6},{6,7},{7,0},{8,9},{9,10},{10,1... | collective-permute-start | bytes 245768 | tf_op jit(solution)/shard_map/ppermute | solution.py:16
  5.2 0.7 multiply_bitcast_fusion.7
  5.9 0.7 multiply_bitcast_fusion.3
  6.6 0.7 subtract_add_fusion
  7.2 0.1 select_reduce_fusion.1
  7.4 2.5 %constant_dynamic-update-slice_fusion.1 = bf16[32,522,128]{2,1,0:T(8,128)(2,1)S(1)} fusion(bf16[32,512,128]{2,1,0:T(8,128)(2,1)} %param.5), kind=kLoop, calls=%fused_computation.118 | loop fusion | bytes 8388608
  9.9 0.0 collective-permute-done.1
  10.0 0.0 collective-permute-done
  10.0 33.9 %multiply_add_fusion = f32[32,512,128]{2,1,0:T(8,128)} fusion(bf16[32,512,128]{2,1,0:T(8,128)(2,1)} %param.5, bf16[32,10,128]{2,1,0:T(8,128)(2,1)S(1)} %collective-permute-done, bf16[32,522,128]{2,1,0:T(8,128)(2,1)S(1)} %constant_dynamic-update-slice_fusion, f32[128]{0:T(128)S(1)} %get-tuple-element.31, f32[128]{0:T(128)S(1)} %get-tuple-element.32, ...), kind=kLoop, calls=%fused_computation.100 | loop fusion | flops 186646528 | bytes 50423808 | tf_op jit(solution)/shard_map/add | solution.py:48
  43.9 3.0 %fusion.64 = (f32[10,512,128]{2,1,0:T(8,128)S(1)}, f32[10,512,128]{2,1,0:T(8,128)S(1)}) fusion(f32[32,512,128]{2,1,0:T(8,128)} %multiply_add_fusion), kind=kLoop, calls=%fused_computation.176 | loop fusion | bytes 10485760 | tf_op jit(solution)/shard_map/slice | solution.py:13
  46.9 0.1 collective-permute-start.2
  47.0 6.4 %collective-permute-start.3 = (f32[10,512,128]{2,1,0:T(8,128)S(1)}, f32[10,512,128]{2,1,0:T(8,128)S(1)}, u32[]{:S(2)}, u32[]{:S(2)}) collective-permute-start(f32[10,512,128]{2,1,0:T(8,128)S(1)} %get-tuple-element.8), channel_id=1, source_target_pairs={{8,0},{16,8},{24,16},{32,24},{40,32},{48,40},{56,48},{64,56},{72,6... | collective-permute-start | bytes 7864328 | tf_op jit(solution)/shard_map/ppermute | solution.py:18
  53.4 29.2 %collective-permute-done.2 = f32[10,512,128]{2,1,0:T(8,128)S(1)} collective-permute-done((f32[10,512,128]{2,1,0:T(8,128)S(1)}, f32[10,512,128]{2,1,0:T(8,128)S(1)}, u32[]{:S(2)}, u32[]{:S(2)}) %collective-permute-start.2) | collective-permute-done | bytes 2621472 | tf_op jit(solution)/shard_map/ppermute | solution.py:16
  82.6 0.0 collective-permute-done.3
  82.6 57.6 %fusion.3 = f32[32,512,128]{2,1,0:T(8,128)} fusion(f32[32,512,128]{2,1,0:T(8,128)} %multiply_add_fusion, f32[10,512,128]{2,1,0:T(8,128)S(1)} %collective-permute-done.3, f32[10,512,128]{2,1,0:T(8,128)S(1)} %collective-permute-done.2, f32[128]{0:T(128)S(1)} %get-tuple-element.12, f32[128]{0:T(128)S(1)} %get-tuple-element.13, f32[128]{0:T(128)S(1)} %get-tuple-element.14, ...), kind=kLoop, calls=%fused_computation.46 | loop fusion | flops 121634816 | bytes 22030336 | tf_op jit(solution)/shard_map/add | solution.py:48
  (7 shorter events, 0.1 us)
Async XLA Ops:
  1.0 8.9 %collective-permute-start.1 = (bf16[32,10,128]{2,1,0:T(8,128)(2,1)S(1)}, bf16[32,10,128]{2,1,0:T(8,128)(2,1)S(1)}, u32[]{:S(2)}, u32[]{:S(2)}) collective-permute-start(bf16[32,10,128]{2,1,0:T(8,128)(2,1)S(1)} %get-tuple-element.9), channel_id=1, source_target_pairs={{1,0},{2,1},{3,2},{4,3},{5,4},{6,5},{7,6},{0,7},{9,8},{10,9},{11,1... | collective-permute-start | bytes 245768 | tf_op jit(solution)/shard_map/ppermute | solution.py:18
  1.6 8.3 %collective-permute-start = (bf16[32,10,128]{2,1,0:T(8,128)(2,1)S(1)}, bf16[32,10,128]{2,1,0:T(8,128)(2,1)S(1)}, u32[]{:S(2)}, u32[]{:S(2)}) collective-permute-start(bf16[32,10,128]{2,1,0:T(8,128)(2,1)S(1)} %get-tuple-element.10), channel_id=1, source_target_pairs={{0,1},{1,2},{2,3},{3,4},{4,5},{5,6},{6,7},{7,0},{8,9},{9,10},{10,1... | collective-permute-start | bytes 245768 | tf_op jit(solution)/shard_map/ppermute | solution.py:16
  46.9 35.7 %collective-permute-start.2 = (f32[10,512,128]{2,1,0:T(8,128)S(1)}, f32[10,512,128]{2,1,0:T(8,128)S(1)}, u32[]{:S(2)}, u32[]{:S(2)}) collective-permute-start(f32[10,512,128]{2,1,0:T(8,128)S(1)} %get-tuple-element.7), channel_id=1, source_target_pairs={{0,8},{8,16},{16,24},{24,32},{32,40},{40,48},{48,56},{56,64},{64,7... | collective-permute-start | bytes 7864328 | tf_op jit(solution)/shard_map/ppermute | solution.py:16
  47.0 35.6 %collective-permute-start.3 = (f32[10,512,128]{2,1,0:T(8,128)S(1)}, f32[10,512,128]{2,1,0:T(8,128)S(1)}, u32[]{:S(2)}, u32[]{:S(2)}) collective-permute-start(f32[10,512,128]{2,1,0:T(8,128)S(1)} %get-tuple-element.8), channel_id=1, source_target_pairs={{8,0},{16,8},{24,16},{32,24},{40,32},{48,40},{56,48},{64,56},{72,6... | collective-permute-start | bytes 7864328 | tf_op jit(solution)/shard_map/ppermute | solution.py:18
where the time goes:
time: 143 us; the launch traced here: 140 us
  other arithmetic  93.7 us (66%)
  waiting for transfers between devices  29.2 us (20%)
  starting transfers between devices  10.7 us (7%)
  local copies, waits for them, and re-layouts  6.56 us (5%)
    add x2, other arithmetic, sweep(): total = total + coef[index][None, None, :] * piece.astype(jnp.float32)  91.5 us
    ppermute x2, waiting for transfers between devices, with_halo(): lax.ppermute(tail, axis, [(i, (i + 1) % count) for i in range(count)])  29.2 us
    ppermute x2, starting transfers between devices, with_halo(): lax.ppermute(head, axis, [((i + 1) % count, i) for i in range(count)])  6.98 us
    ppermute x2, starting transfers between devices, with_halo(): lax.ppermute(tail, axis, [(i, (i + 1) % count) for i in range(count)])  3.68 us
    slice x1, local copies, waits for them, and re-layouts, with_halo(): lax.slice_in_dim(cells, cells.shape[dim] - width, cells.shape[dim], axis=...  3 us
  transfers between devices with their start and end apart: 4, of which 1 were waited for; matrix products, arithmetic and copies ran while one was open for 3% of the time, Pallas kernels for 0%

commit v1 on v0

v1 whole, which is shorter than its diff:
```python
import functools
import jax
import jax.numpy as jnp
from jax import lax
from jax.experimental import pallas as pl
from jax.experimental.pallas import tpu as pltpu
from jax.sharding import PartitionSpec as P

REACH = 8
TOP = REACH + 2
BOT = REACH + 1
PAD = 16
LANES = 128
STEP = 128
MESH = pl.DeviceIdType.MESH


def lagrange(t):
    return (
        -t * (t - 1.0) * (t - 2.0) / 6.0,
        (t + 1.0) * (t - 1.0) * (t - 2.0) / 2.0,
        -(t + 1.0) * t * (t - 2.0) / 2.0,
        (t + 1.0) * t * (t - 1.0) / 6.0,
    )


def rows_needed(shift):
    return jnp.clip(2 - shift, 0, TOP), jnp.clip(shift + 1, 0, BOT)


def build_table(table, shift, count, depth, slots):
    f32 = jnp.float32
    need = count.astype(f32)
    wide = jnp.broadcast_to(need, (16, LANES))
    level = lax.broadcasted_iota(jnp.int32, (16, LANES), 0).astype(f32)
    inside = wide > level
    before = jnp.sum(jnp.minimum(wide, level), axis=1, keepdims=True)
    row = lax.broadcasted_iota(jnp.int32, (LANES, LANES), 0)
    col = lax.broadcasted_iota(jnp.int32, (LANES, LANES), 1)
    upper = jnp.where(row < col, 1.0, 0.0).astype(jnp.bfloat16)
    rank = jnp.dot(
        jnp.where(inside, 1.0, 0.0).astype(jnp.bfloat16), upper, preferred_element_type=f32
    )
    place = jnp.where(inside, before + rank, -1.0)
    lane = row.astype(f32)
    for h in range(depth):
        line = jnp.broadcast_to(place[h : h + 1, :], (LANES, LANES))
        for p in range(slots):
            hit = jnp.where(line == lane + float(p * LANES), 1.0, 0.0)
            table[p * LANES : (p + 1) * LANES, h * LANES : (h + 1) * LANES] = hit.astype(jnp.bfloat16)


def x_tile(xs, mid, y, unit, wx, first, last, low, high):
    m16 = unit >= 16.0
    m8 = unit >= 8.0
    left = jnp.where(m16, unit - 16.0, jnp.where(m8, unit - 8.0, unit))
    m4 = left >= 4.0
    left = jnp.where(m4, left - 4.0, left)
    m2 = left >= 2.0
    left = jnp.where(m2, left - 2.0, left)
    m1 = left >= 1.0

    def source(r):
        return xs[min(max(r, low), high), pl.ds(y, 16), :]

    @functools.cache
    def by8(j):
        return jnp.where(m16, source(j + 16), jnp.where(m8, source(j + 8), source(j)))

    @functools.cache
    def by4(j):
        return jnp.where(m4, by8(j + 4), by8(j))

    @functools.cache
    def by2(j):
        return jnp.where(m2, by4(j + 2), by4(j))

    @functools.cache
    def by1(j):
        return jnp.where(m1, by2(j + 1), by2(j)).astype(jnp.float32)

    for i in range(first, last):
        mid[i, pl.ds(y, 16), :] = (
            wx[0] * by1(i + 3) + wx[1] * by1(i + 2) + wx[2] * by1(i + 1) + wx[3] * by1(i)
        )


def y_row(mid, out, i, start, count, strip, turn, minus, plus, wy):
    tiles = count // 8
    base = start + PAD

    @functools.cache
    def turned(j):
        return jnp.take_along_axis(mid[i, pl.ds(base + 8 * j, 8), :], turn, axis=0)

    for j in range(-1, tiles + 1):
        strip[pl.ds(8 * (j + 1), 8), :] = jnp.where(
            minus, turned(j - 1), jnp.where(plus, turned(j + 1), turned(j))
        )
    for j in range(tiles):
        b = 8 * (j + 1)
        out[i, pl.ds(start + 8 * j, 8), :] = (
            wy[0] * strip[pl.ds(b + 1, 8), :]
            + wy[1] * strip[pl.ds(b, 8), :]
            + wy[2] * strip[pl.ds(b - 1, 8), :]
            + wy[3] * strip[pl.ds(b - 2, 8), :]
        )


def kernel(dims, slots, x_hbm, sx_ref, sy_ref, fx_ref, fy_ref, out, xs, mid, strip, *rest):
    rows, cols, nx, ny = dims
    if slots:
        table, send, recv, load_sem, x_send, x_recv, y_send, y_recv, c_send, c_recv = rest
    else:
        load_sem, x_send, x_recv, y_send, y_recv, c_send, c_recv = rest
    gx, gy = lax.axis_index("gx"), lax.axis_index("gy")
    xm, xp = lax.rem(gx + nx - 1, nx), lax.rem(gx + 1, nx)
    ym, yp = lax.rem(gy + ny - 1, ny), lax.rem(gy + 1, ny)

    loads = [
        pltpu.make_async_copy(x_hbm.at[pl.ds(a, n)], xs.at[pl.ds(TOP + a, n), pl.ds(PAD, cols), :], load_sem.at[k])
        for k, (a, n) in enumerate(((rows - TOP, TOP), (0, TOP), (TOP, rows - 2 * TOP)))
    ]
    for load in loads:
        load.start()
    barrier = pltpu.get_barrier_semaphore()
    for a in (xm, gx, xp):
        for b in (ym, gy, yp):
            if a is gx and b is gy:
                continue
            pl.semaphore_signal(barrier, inc=1, device_id=(a, b), device_id_type=MESH)

    counts = rows_needed(sx_ref[...])
    if slots:
        for d in range(2):
            build_table(table.at[d], sx_ref[...], counts[d], (TOP, BOT)[d], slots)
    unit = jnp.broadcast_to((sx_ref[...] + REACH).astype(jnp.float32), (16, LANES)).astype(jnp.bfloat16)
    wx = [jnp.broadcast_to(w, (16, LANES)) for w in lagrange(fx_ref[...])]
    wy = [jnp.broadcast_to(w, (8, LANES)) for w in lagrange(fy_ref[...])]
    tot = lax.broadcasted_iota(jnp.int32, (8, LANES), 0) + jnp.broadcast_to(sy_ref[...], (8, LANES))
    turn, minus, plus = (tot + 16) & 7, tot < 0, tot >= 8

    edges = [0] + [STEP * (k + 1) + PAD for k in range(cols // STEP - 1)] + [cols]
    n = len(edges) - 1
    mine = ([rows - 1 - h + TOP for h in range(TOP)], [TOP + h for h in range(BOT)])
    theirs = ([TOP - 1 - h for h in range(TOP)], [TOP + rows + h for h in range(BOT)])

    def pack(k):
        a, w = edges[k], edges[k + 1] - edges[k]
        for d in range(2):
            block = jnp.concatenate([xs[r, pl.ds(PAD + a, w), :] for r in mine[d]], axis=1)
            packed = lax.dot_general(
                block, table[d][:, : len(mine[d]) * LANES], (((1,), (1,)), ((), ())), preferred_element_type=jnp.float32
            )
            for p in range(slots):
                send[d, p, pl.ds(a, w), :] = packed[:, p * LANES : (p + 1) * LANES].astype(jnp.bfloat16)

    def unpack(a, w):
        for d in range(2):
            block = jnp.concatenate([recv[d, p, pl.ds(a, w), :] for p in range(slots)], axis=1)
            found = jnp.dot(block, table[d][:, : len(mine[d]) * LANES], preferred_element_type=jnp.float32)
            for h, r in enumerate(theirs[d]):
                xs[r, pl.ds(a, w), :] = found[:, h * LANES : (h + 1) * LANES].astype(jnp.bfloat16)

    def halo(d, a, w, to):
        if slots:
            return send.at[d, :, pl.ds(a, w), :], recv.at[d, :, pl.ds(to, w), :]
        r0, count = ((rows, TOP), (TOP, BOT))[d]
        s0 = (0, TOP + rows)[d]
        return xs.at[pl.ds(r0, count), pl.ds(PAD + a, w), :], xs.at[pl.ds(s0, count), pl.ds(to, w), :]

    def remote(src, dst, ssem, rsem, to):
        return pltpu.make_async_remote_copy(
            src_ref=src, dst_ref=dst, send_sem=ssem, recv_sem=rsem, device_id=to, device_id_type=MESH
        )

    xto = (xp, xm)
    x_copies = [
        [
            remote(*halo(d, edges[k], edges[k + 1] - edges[k], PAD + edges[k]), x_send.at[d, k], x_recv.at[d, k], (xto[d], gy))
            for d in range(2)
        ]
        for k in range(n)
    ]
    y_copies = [
        remote(
            x_hbm.at[:, pl.ds((cols - PAD, 0)[s], PAD), :],
            xs.at[pl.ds(TOP, rows), pl.ds((0, PAD + cols)[s], PAD), :],
            y_send.at[s], y_recv.at[s], (gx, (yp, ym)[s]),
        )
        for s in range(2)
    ]
    c_copies = [
        [
            remote(*halo(d, (cols - PAD, 0)[s], PAD, (0, PAD + cols)[s]), c_send.at[d, s], c_recv.at[d, s], (xto[d], (yp, ym)[s]))
            for d in range(2)
        ]
        for s in range(2)
    ]

    loads[0].wait()
    loads[1].wait()
    if slots:
        pack(0)
    pl.semaphore_wait(barrier, 8)
    for k in range(n):
        if slots and k:
            pack(k)
        for c in x_copies[k]:
            c.start()
        if k == 0:
            for c in y_copies:
                c.start()
            for c in c_copies[1]:
                c.start()
        if k == n - 1:
            for c in c_copies[0]:
                c.start()
    loads[2].wait()

    def x_tiles(first, last, low, high, t0, t1):
        def step(t, carry):
            x_tile(xs, mid, pl.multiple_of(t * 16, 16), unit, wx, first, last, low, high)
            return carry

        lax.fori_loop(t0, t1, step, 0)

    def y_rows(row_of, count, start, width):
        def step(q, carry):
            y_row(mid, out, row_of(q), start, width, strip.at[q & 1], turn, minus, plus, wy)
            return carry

        lax.fori_loop(0, count, step, 0)

    inner0, inner1 = TOP, rows - BOT
    for c in y_copies:
        c.wait_recv()
    x_tiles(inner0, inner1, TOP, TOP + rows - 1, 0, (cols + 2 * PAD) // 16)
    for k in range(cols // STEP):
        y_rows(lambda q: q + inner0, inner1 - inner0, k * STEP, STEP)

    for k in range(n):
        for c in x_copies[k]:
            c.wait_recv()
        for s in range(2):
            if k == (0, n - 1)[s]:
                for c in c_copies[s]:
                    c.wait_recv()
        a = 0 if k == 0 else PAD + edges[k]
        b = PAD + edges[k + 1] if k < n - 1 else cols + 2 * PAD
        if slots:
            unpack(a, b - a)
        top = TOP + rows + BOT - 1
        x_tiles(0, inner0, 0, top, a // 16, b // 16)
        x_tiles(inner1, rows, 0, top, a // 16, b // 16)
        y_rows(lambda q: q, inner0, k * STEP, STEP)
        y_rows(lambda q: q + inner1, rows - inner1, k * STEP, STEP)

    for group in (*x_copies, y_copies, *c_copies):
        for c in group:
            c.wait_send()


def exchange_and_sweep(slots, collective_id, nx, ny, cells, sx, sy, fx, fy):
    rows, cols, lanes = cells.shape
    n = cols // STEP
    dma = pltpu.SemaphoreType.DMA
    scratch = [
        pltpu.VMEM((rows + TOP + BOT, cols + 2 * PAD, lanes), jnp.bfloat16),
        pltpu.VMEM((rows, cols + 2 * PAD, lanes), jnp.float32),
        pltpu.VMEM((2, STEP + 16, lanes), jnp.float32),
    ]
    if slots:
        scratch += [
            pltpu.VMEM((2, slots * lanes, TOP * lanes), jnp.bfloat16),
            pltpu.VMEM((2, slots, cols, lanes), jnp.bfloat16),
            pltpu.VMEM((2, slots, cols + 2 * PAD, lanes), jnp.bfloat16),
        ]
    scratch += [dma((3,)), dma((2, n)), dma((2, n)), dma((2,)), dma((2,)), dma((2, 2)), dma((2, 2))]
    vmem = pl.BlockSpec(memory_space=pltpu.VMEM)
    return pl.pallas_call(
        functools.partial(kernel, (rows, cols, nx, ny), slots),
        out_shape=jax.ShapeDtypeStruct((rows, cols, lanes), jnp.float32),
        in_specs=[pl.BlockSpec(memory_space=pl.ANY)] + [vmem] * 4,
        out_specs=vmem,
        scratch_shapes=scratch,
        compiler_params=pltpu.CompilerParams(
            vmem_limit_bytes=56 * 1024 * 1024, collective_id=collective_id, has_side_effects=True
        ),
    )(cells, *(a.reshape(1, lanes) for a in (sx, sy, fx, fy)))


def solution(mesh):
    nx, ny = mesh.shape["gx"], mesh.shape["gy"]
    return jax.shard_map(
        functools.partial(exchange_and_sweep, 0, 0, nx, ny),
        mesh=mesh,
        in_specs=(P("gx", "gy", None), P(), P(), P(), P()),
        out_specs=P("gx", "gy", None),
        check_vma=False,
    )
```

time: 143 us -> 48.4 us (0.34); the launches traced: 140 us -> 48.3 us
  other arithmetic: 93.7 us -> 0 us
  Pallas kernels: 0 us -> 40.6 us
  waiting for transfers between devices: 29.2 us -> 0 us
  starting transfers between devices: 10.7 us -> 0 us
    add x3 -> x0, other arithmetic: 92.2 us -> none  [the longest x2 91.5 us: sweep(): total = total + coef[index][None, None, :] * piece.astype(jnp.float32)]
    pallas_call x0 -> x1, Pallas kernels: none -> 40.6 us  [exchange_and_sweep(): pl.pallas_call(functools.partial(kernel, (rows, cols, nx, ny), slots), ou...]
    ppermute x4 -> x0, waiting for transfers between devices: 29.2 us -> none  [the longest x2 29.2 us: with_halo(): lax.ppermute(tail, axis, [(i, (i + 1) % count) for i in range(count)])]
    ppermute x4 -> x0, starting transfers between devices: 10.7 us -> none  [the longest x2 6.98 us: with_halo(): lax.ppermute(head, axis, [((i + 1) % count, i) for i in range(count)])]
    unnamed x1, local copies, waits for them, and re-layouts: 2.5 us -> 7.69 us
    slice x2 -> x0, local copies, waits for them, and re-layouts: 4.01 us -> none  [the longest x1 3 us: with_halo(): lax.slice_in_dim(cells, cells.shape[dim] - width, cells.shape[dim], axis=...]
  transfers between devices with their start and end apart: 4 -> 0, of which waited for: 1 -> 0; matrix products, arithmetic and copies ran while one was open for 3% -> 0% of each run, Pallas kernels for 0% -> 0%
where the time goes in v1:
time: 48.4 us; the launch traced here: 48.3 us
  Pallas kernels  40.6 us (84%)
  local copies, waits for them, and re-layouts  7.69 us (16%)
    pallas_call x1, Pallas kernels, exchange_and_sweep(): pl.pallas_call(functools.partial(kernel, (rows, cols, nx, ny), slots), ou...  40.6 us
    unnamed x1, local copies, waits for them, and re-layouts  7.69 us

profile of v1, /device:TPU:26, one launch (start us, length us, event | category | flops | bytes accessed | tf_op | source)
XLA Modules:
  0.0 48.3 jit_solution(11113798688524258197)
XLA Ops:
  0.0 40.6 %shard_map.55 = f32[32,512,128]{2,1,0:T(8,128)} custom-call(bf16[32,512,128]{2,1,0:T(8,128)(2,1)} %x_hbm.1, s32[1,128]{1,0:T(1,128)} %bitcast.4, s32[1,128]{1,0:T(1,128)} %bitcast.5, f32[1,128]{1,0:T(1,128)} %bitcast.6, f32[1,128]{1,0:T(1,128)} %bitcast.7), custom_call_target="tpu_custom_call" | custom-call | tf_op jit(solution)/shard_map/pallas_call | solution.py:281
  40.6 7.7 %copy.7 = f32[32,512,128]{2,1,0:T(8,128)} copy(f32[32,512,128]{2,1,0:T(8,128)} %shard_map.55) | data formatting | bytes 16777216

commit v2 on v1

v2 whole, which is shorter than its diff:
```python
import functools
import jax
import jax.numpy as jnp
from jax import lax
from jax.experimental import pallas as pl
from jax.experimental.pallas import tpu as pltpu
from jax.sharding import PartitionSpec as P

REACH = 8
TOP = REACH + 2
BOT = REACH + 1
PAD = 16
LANES = 128
STEP = 128
SLOTS = 4
CHUNKS = 4
MESH = pl.DeviceIdType.MESH


def lagrange(t):
    return (
        -t * (t - 1.0) * (t - 2.0) / 6.0,
        (t + 1.0) * (t - 1.0) * (t - 2.0) / 2.0,
        -(t + 1.0) * t * (t - 2.0) / 2.0,
        (t + 1.0) * t * (t - 1.0) / 6.0,
    )


def rows_needed(shift):
    return jnp.clip(2 - shift, 0, TOP), jnp.clip(shift + 1, 0, BOT)


def build_table(table, count, depth, slots):
    f32 = jnp.float32
    need = count.astype(f32)
    wide = jnp.broadcast_to(need, (16, LANES))
    level = lax.broadcasted_iota(jnp.int32, (16, LANES), 0).astype(f32)
    inside = wide > level
    before = jnp.sum(jnp.minimum(wide, level), axis=1, keepdims=True)
    row = lax.broadcasted_iota(jnp.int32, (LANES, LANES), 0)
    col = lax.broadcasted_iota(jnp.int32, (LANES, LANES), 1)
    upper = jnp.where(row < col, 1.0, 0.0).astype(jnp.bfloat16)
    rank = jnp.dot(
        jnp.where(inside, 1.0, 0.0).astype(jnp.bfloat16), upper, preferred_element_type=f32
    )
    place = jnp.where(inside, before + rank, -1.0)
    lane = row.astype(f32)
    for h in range(depth):
        line = jnp.broadcast_to(place[h : h + 1, :], (LANES, LANES))
        for p in range(slots):
            hit = jnp.where(line == lane + float(p * LANES), 1.0, 0.0)
            table[p * LANES : (p + 1) * LANES, h * LANES : (h + 1) * LANES] = hit.astype(jnp.bfloat16)


def chunk_edges(total):
    tiles = total // 16
    return [16 * (tiles * k // CHUNKS) for k in range(CHUNKS + 1)]


def x_tile(xs, mid, y, to, unit, wx, first, last, low, high):
    m16 = unit >= 16.0
    m8 = unit >= 8.0
    left = jnp.where(m16, unit - 16.0, jnp.where(m8, unit - 8.0, unit))
    m4 = left >= 4.0
    left = jnp.where(m4, left - 4.0, left)
    m2 = left >= 2.0
    left = jnp.where(m2, left - 2.0, left)
    m1 = left >= 1.0

    def source(r):
        return xs[min(max(r, low), high), pl.ds(y, 16), :]

    @functools.cache
    def by8(j):
        return jnp.where(m16, source(j + 16), jnp.where(m8, source(j + 8), source(j)))

    @functools.cache
    def by4(j):
        return jnp.where(m4, by8(j + 4), by8(j))

    @functools.cache
    def by2(j):
        return jnp.where(m2, by4(j + 2), by4(j))

    @functools.cache
    def by1(j):
        return jnp.where(m1, by2(j + 1), by2(j)).astype(jnp.float32)

    for i in range(first, last):
        mid[i, pl.ds(to, 16), :] = (
            wx[0] * by1(i + 3) + wx[1] * by1(i + 2) + wx[2] * by1(i + 1) + wx[3] * by1(i)
        )


def y_row(mid, out, i, start, count, strip, turn, minus, plus, wy):
    tiles = count // 8
    base = start + PAD

    @functools.cache
    def turned(j):
        return jnp.take_along_axis(mid[i, pl.ds(base + 8 * j, 8), :], turn, axis=0)

    for j in range(-1, tiles + 1):
        strip[pl.ds(8 * (j + 1), 8), :] = jnp.where(
            minus, turned(j - 1), jnp.where(plus, turned(j + 1), turned(j))
        )
    for j in range(tiles):
        b = 8 * (j + 1)
        out[i, pl.ds(start + 8 * j, 8), :] = (
            wy[0] * strip[pl.ds(b + 1, 8), :]
            + wy[1] * strip[pl.ds(b, 8), :]
            + wy[2] * strip[pl.ds(b - 1, 8), :]
            + wy[3] * strip[pl.ds(b - 2, 8), :]
        )


def exchange(dims, slots, x_hbm, sx_hbm, sy_hbm, fx_hbm, mid, load, sx_ref, sy_ref, fx_ref, xs, y_out, y_in, *rest):
    rows, cols, nx, ny = dims
    if slots:
        table, send, recv, y_table, y_send_buf, y_recv_buf, load_sem, x_send, x_recv, y_send, y_recv = rest
    else:
        load_sem, x_send, x_recv, y_send, y_recv = rest
    gx, gy = lax.axis_index("gx"), lax.axis_index("gy")
    xm, xp = lax.rem(gx + nx - 1, nx), lax.rem(gx + 1, nx)
    ym, yp = lax.rem(gy + ny - 1, ny), lax.rem(gy + 1, ny)
    total = cols + 2 * PAD

    loads = [
        pltpu.make_async_copy(x_hbm.at[pl.ds(a, c)], xs.at[pl.ds(TOP + a, c), pl.ds(0, cols), :], load_sem.at[k])
        for k, (a, c) in enumerate(((rows - TOP, TOP), (0, TOP), (TOP, rows - 2 * TOP)))
    ]
    y_loads = [
        pltpu.make_async_copy(x_hbm.at[:, pl.ds((0, cols - PAD)[s], PAD), :], y_out.at[s], load_sem.at[3 + s])
        for s in range(2)
    ]
    small = [
        pltpu.make_async_copy(src, dst, load_sem.at[5 + k])
        for k, (src, dst) in enumerate(((sx_hbm, sx_ref), (sy_hbm, sy_ref), (fx_hbm, fx_ref)))
    ]
    for c in (*small, loads[0], loads[1], *y_loads, loads[2]):
        c.start()
    barrier = pltpu.get_barrier_semaphore()
    for to in ((xm, gy), (xp, gy), (gx, ym), (gx, yp)):
        pl.semaphore_signal(barrier, inc=1, device_id=to, device_id_type=MESH)

    for c in small:
        c.wait()
    if slots:
        for d, need in enumerate(rows_needed(sx_ref[...])):
            build_table(table.at[d], need, (TOP, BOT)[d], slots)
    unit = jnp.broadcast_to((sx_ref[...] + REACH).astype(jnp.float32), (16, LANES)).astype(jnp.bfloat16)
    wx = [jnp.broadcast_to(w, (16, LANES)) for w in lagrange(fx_ref[...])]

    edges = chunk_edges(total)
    n = len(edges) - 1
    mine = ([rows - 1 - h + TOP for h in range(TOP)], [TOP + h for h in range(BOT)])
    theirs = ([TOP - 1 - h for h in range(TOP)], [TOP + rows + h for h in range(BOT)])

    def squeeze(lines, lookup, to):
        block = jnp.concatenate(lines, axis=1)
        packed = lax.dot_general(
            block, lookup[:, : len(lines) * LANES], (((1,), (1,)), ((), ())), preferred_element_type=jnp.float32
        )
        for p in range(slots):
            to(p, packed[:, p * LANES : (p + 1) * LANES].astype(jnp.bfloat16))

    def spread(packed, lookup, depth):
        found = jnp.dot(jnp.concatenate(packed, axis=1), lookup[:, : depth * LANES], preferred_element_type=jnp.float32)
        return [found[:, h * LANES : (h + 1) * LANES] for h in range(depth)]

    def pack(k, d):
        a, w = edges[k], edges[k + 1] - edges[k]

        def put(p, value):
            send[d, p, pl.ds(a, w), :] = value

        squeeze([xs[r, pl.ds(a, w), :] for r in mine[d]], table[d], put)

    def pack_y(s):
        def put(p, value):
            y_send_buf[s, p] = value

        by_column = jnp.swapaxes(y_out[s].astype(jnp.float32), 0, 1).astype(jnp.bfloat16)
        order = ([h for h in range(BOT)], [PAD - 1 - h for h in range(TOP)])[s]
        squeeze([by_column[j] for j in order], y_table[s], put)

    def unpack_y(s):
        depth = (BOT, TOP)[s]
        lines = spread([y_recv_buf[s, p] for p in range(slots)], y_table[s], depth)
        zero = jnp.zeros_like(lines[0])
        lines = lines + [zero] * (PAD - depth)
        block = jnp.stack(lines if s == 0 else lines[::-1], axis=0)
        y_in[s] = jnp.swapaxes(block, 0, 1).astype(jnp.bfloat16)

    def unpack(k):
        a, w = edges[k], edges[k + 1] - edges[k]
        for d in range(2):
            lines = spread([recv[d, p, pl.ds(a, w), :] for p in range(slots)], table[d], len(theirs[d]))
            for r, line in zip(theirs[d], lines):
                xs[r, pl.ds(a, w), :] = line.astype(jnp.bfloat16)

    def halo(d, k):
        part = pl.ds(edges[k], edges[k + 1] - edges[k])
        if slots:
            return send.at[d, :, part, :], recv.at[d, :, part, :]
        r0, c = ((rows, TOP), (TOP, BOT))[d]
        return xs.at[pl.ds(r0, c), part, :], xs.at[pl.ds((0, TOP + rows)[d], c), part, :]

    def remote(src, dst, ssem, rsem, to):
        return pltpu.make_async_remote_copy(
            src_ref=src, dst_ref=dst, send_sem=ssem, recv_sem=rsem, device_id=to, device_id_type=MESH
        )

    x_copies = [
        [remote(*halo(d, k), x_send.at[d, k], x_recv.at[d, k], ((xp, xm)[d], gy)) for d in range(2)] for k in range(n)
    ]
    y_from, y_to = (y_send_buf, y_recv_buf) if slots else (y_out, y_in)
    y_copies = [remote(y_from.at[s], y_to.at[s], y_send.at[s], y_recv.at[s], (gx, (ym, yp)[s])) for s in range(2)]

    loads[0].wait()
    if slots:
        pack(0, 0)
    pl.semaphore_wait(barrier, 4)
    x_copies[0][0].start()
    loads[1].wait()
    if slots:
        pack(0, 1)
    x_copies[0][1].start()
    for c in y_loads:
        c.wait()
    if slots:
        for s, need in enumerate(rows_needed(sy_ref[...])[::-1]):
            build_table(y_table.at[s], need, (BOT, TOP)[s], slots)
            pack_y(s)
    for c in y_copies:
        c.start()
    for k in range(1, n):
        if k == n - 1:
            loads[2].wait()
            for s in range(2):
                y_copies[s].wait_recv()
                if slots:
                    unpack_y(s)
                xs[TOP : TOP + rows, cols + PAD * s : cols + PAD * (s + 1), :] = y_in[s]
        for d in range(2):
            if slots:
                pack(k, d)
            x_copies[k][d].start()

    def x_tiles(first, last, low, high, t0, t1):
        def step(t, carry):
            y = pl.multiple_of(t * 16, 16)
            to = pl.multiple_of(lax.rem(t + 1, total // 16) * 16, 16)
            x_tile(xs, mid, y, to, unit, wx, first, last, low, high)
            return carry

        lax.fori_loop(t0, t1, step, 0)

    needs = [jnp.sum(need.astype(jnp.float32)) for ref in (sx_ref, sy_ref) for need in rows_needed(ref[...])]
    load[0] = functools.reduce(jnp.maximum, needs)

    inner0, inner1 = TOP, rows - BOT
    x_tiles(inner0, inner1, TOP, TOP + rows - 1, 0, total // 16)

    top = TOP + rows + BOT - 1
    for k in range(n):
        for c in x_copies[k]:
            c.wait_recv()
        if slots:
            unpack(k)
        x_tiles(0, inner0, 0, top, edges[k] // 16, edges[k + 1] // 16)
        x_tiles(inner1, rows, 0, top, edges[k] // 16, edges[k + 1] // 16)

    for group in (*x_copies, y_copies):
        for c in group:
            c.wait_send()


def finish(dims, mid, sy_ref, fy_ref, out, strip, rows_out, sem):
    rows, cols = dims
    wy = [jnp.broadcast_to(w, (8, LANES)) for w in lagrange(fy_ref[...])]
    tot = lax.broadcasted_iota(jnp.int32, (8, LANES), 0) + jnp.broadcast_to(sy_ref[...], (8, LANES))
    turn, minus, plus = (tot + 16) & 7, tot < 0, tot >= 8
    per = cols // STEP

    def drain(i):
        return pltpu.make_async_copy(rows_out.at[i], out.at[i], sem.at[i])

    def step(i, carry):
        for k in range(per):
            y_row(mid, rows_out, i, k * STEP, STEP, strip.at[k % 2], turn, minus, plus, wy)
        drain(i).start()
        return carry

    lax.fori_loop(0, rows, step, 0)

    def end(i, carry):
        drain(i).wait()
        return carry

    lax.fori_loop(0, rows, end, 0)


def sweep_x(slots, collective_id, nx, ny, cells, sx, sy, fx):
    rows, cols, lanes = cells.shape
    n, total = CHUNKS, cols + 2 * PAD
    dma = pltpu.SemaphoreType.DMA
    bf16 = jnp.bfloat16
    scratch = [
        pltpu.VMEM((1, lanes), jnp.int32),
        pltpu.VMEM((1, lanes), jnp.int32),
        pltpu.VMEM((1, lanes), jnp.float32),
        pltpu.VMEM((rows + TOP + BOT, total, lanes), bf16),
        pltpu.VMEM((2, rows, PAD, lanes), bf16),
        pltpu.VMEM((2, rows, PAD, lanes), bf16),
    ]
    if slots:
        scratch += [
            pltpu.VMEM((2, slots * lanes, TOP * lanes), bf16),
            pltpu.VMEM((2, slots, total, lanes), bf16),
            pltpu.VMEM((2, slots, total, lanes), bf16),
            pltpu.VMEM((2, slots * lanes, TOP * lanes), bf16),
            pltpu.VMEM((2, slots, rows, lanes), bf16),
            pltpu.VMEM((2, slots, rows, lanes), bf16),
        ]
    scratch += [dma((8,)), dma((2, n)), dma((2, n)), dma((2,)), dma((2,))]
    vmem = pl.BlockSpec(memory_space=pltpu.VMEM)
    return pl.pallas_call(
        functools.partial(exchange, (rows, cols, nx, ny), slots),
        out_shape=(
            pltpu.VMEM((rows, total, lanes), jnp.float32),
            jax.ShapeDtypeStruct((1,), jnp.float32),
        ),
        in_specs=[pl.BlockSpec(memory_space=pltpu.HBM)] * 4,
        out_specs=(vmem, pl.BlockSpec(memory_space=pltpu.SMEM)),
        scratch_shapes=scratch,
        compiler_params=pltpu.CompilerParams(
            vmem_limit_bytes=52 * 1024 * 1024, collective_id=collective_id, has_side_effects=True
        ),
    )(cells, sx, sy, fx)


def sweep_y(mid, sy, fy):
    rows, total, lanes = mid.shape
    cols = total - 2 * PAD
    dma = pltpu.SemaphoreType.DMA
    vmem = pl.BlockSpec(memory_space=pltpu.VMEM)
    return pl.pallas_call(
        functools.partial(finish, (rows, cols)),
        out_shape=pltpu.HBM((rows, cols, lanes), jnp.float32),
        in_specs=[vmem] * 3,
        out_specs=pl.BlockSpec(memory_space=pltpu.HBM),
        scratch_shapes=[
            pltpu.VMEM((2, STEP + 16, lanes), jnp.float32),
            pltpu.VMEM((rows, cols, lanes), jnp.float32),
            dma((rows,)),
        ],
        compiler_params=pltpu.CompilerParams(vmem_limit_bytes=24 * 1024 * 1024),
    )(mid, sy, fy)


def body(nx, ny, cells, sx, sy, fx, fy):
    sx, sy, fx, fy = (a.reshape(1, LANES) for a in (sx, sy, fx, fy))
    mid, load = sweep_x(SLOTS, 0, nx, ny, cells, sx, sy, fx)

    out = sweep_y(mid, sy, fy)

    def whole(out):
        return sweep_y(sweep_x(0, 1, nx, ny, cells, sx, sy, fx)[0], sy, fy)

    return lax.cond(load[0] <= SLOTS * LANES, lambda out: out, whole, out)


def solution(mesh):
    return jax.shard_map(
        functools.partial(body, mesh.shape["gx"], mesh.shape["gy"]),
        mesh=mesh,
        in_specs=(P("gx", "gy", None), P(), P(), P(), P()),
        out_specs=P("gx", "gy", None),
        check_vma=False,
    )
```

time: 48.4 us -> 32.3 us (0.67)
  the two profiles are of different devices: /device:TPU:26 before, /device:TPU:0 now
where the time goes in v2:
time: 32.3 us; the launch traced here: 32.2 us
  Pallas kernels  31.6 us (98%)
  between operations  0.63 us (2%)
    pallas_call x1, Pallas kernels, sweep_x(): pl.pallas_call(functools.partial(exchange, (rows, cols, nx, ny), slots),...  26.5 us
    pallas_call x1, Pallas kernels, sweep_y(): pl.pallas_call(functools.partial(finish, (rows, cols)), out_shape=pltpu.H...  5.02 us

profile of v2, /device:TPU:0, one launch (start us, length us, event | category | flops | bytes accessed | tf_op | source)
XLA Modules:
  0.0 32.2 jit_solution(17839103942998677553)
XLA Ops:
  0.0 26.5 %shard_map.57 = (f32[32,544,128]{2,1,0:T(8,128)S(1)}, f32[1]{0:T(128)}) custom-call(bf16[32,512,128]{2,1,0:T(8,128)(2,1)} %x_hbm.1, s32[1,128]{1,0:T(1,128)} %bitcast.8, s32[1,128]{1,0:T(1,128)} %bitcast.5, f32[1,128]{1,0:T(1,128)} %bitcast.10), custom_call_target="tpu_custom_call" | custom-call | tf_op jit(solution)/shard_map/pallas_call | solution.py:328
  27.1 5.0 %shard_map.58 = f32[32,512,128]{2,1,0:T(8,128)} custom-call(f32[32,544,128]{2,1,0:T(8,128)S(1)} %get-tuple-element.28.mid, s32[1,128]{1,0:T(1,128)} %bitcast.6, f32[1,128]{1,0:T(1,128)} %bitcast.12), custom_call_target="tpu_custom_call" | custom-call | tf_op jit(solution)/shard_map/pallas_call | solution.py:348
  (1 shorter events, 0.0 us)

commit v3 on v2

--- a/solution.py
+++ b/solution.py
@@ -44,12 +44,17 @@
         jnp.where(inside, 1.0, 0.0).astype(jnp.bfloat16), upper, preferred_element_type=f32
     )
     place = jnp.where(inside, before + rank, -1.0)
-    lane = row.astype(f32)
-    for h in range(depth):
-        line = jnp.broadcast_to(place[h : h + 1, :], (LANES, LANES))
-        for p in range(slots):
-            hit = jnp.where(line == lane + float(p * LANES), 1.0, 0.0)
-            table[p * LANES : (p + 1) * LANES, h * LANES : (h + 1) * LANES] = hit.astype(jnp.bfloat16)
+    bf16 = jnp.bfloat16
+    lane = lax.broadcasted_iota(jnp.int32, (16, LANES), 0).astype(f32)
+    lanes = [(lane + float(a)).astype(bf16) for a in range(0, LANES, 16)]
+    one, zero = jnp.ones((16, LANES), bf16), jnp.zeros((16, LANES), bf16)
+    for p in range(slots):
+        local = place - float(p * LANES)
+        local = jnp.where((local >= 0.0) & (local < float(LANES)), local, -1.0)
+        for h in range(depth):
+            line = jnp.broadcast_to(local[h : h + 1, :], (16, LANES)).astype(bf16)
+            for m, value in enumerate(lanes):
+                table[pl.ds(p * LANES + 16 * m, 16), h * LANES : (h + 1) * LANES] = jnp.where(line == value, one, zero)
 
 
 def chunk_edges(total):
@@ -100,21 +105,22 @@
     def turned(j):
         return jnp.take_along_axis(mid[i, pl.ds(base + 8 * j, 8), :], turn, axis=0)
 
+    aligned = {}
     for j in range(-1, tiles + 1):
-        strip[pl.ds(8 * (j + 1), 8), :] = jnp.where(
-            minus, turned(j - 1), jnp.where(plus, turned(j + 1), turned(j))
-        )
-    for j in range(tiles):
-        b = 8 * (j + 1)
-        out[i, pl.ds(start + 8 * j, 8), :] = (
+        aligned[j] = jnp.where(minus, turned(j - 1), jnp.where(plus, turned(j + 1), turned(j)))
+        strip[pl.ds(8 * (j + 1), 8), :] = aligned[j]
+        if j < 1:
+            continue
+        b = 8 * j
+        out[i, pl.ds(start + 8 * (j - 1), 8), :] = (
             wy[0] * strip[pl.ds(b + 1, 8), :]
-            + wy[1] * strip[pl.ds(b, 8), :]
+            + wy[1] * aligned[j - 1]
             + wy[2] * strip[pl.ds(b - 1, 8), :]
             + wy[3] * strip[pl.ds(b - 2, 8), :]
         )
 
 
-def exchange(dims, slots, x_hbm, sx_hbm, sy_hbm, fx_hbm, mid, load, sx_ref, sy_ref, fx_ref, xs, y_out, y_in, *rest):
+def exchange(dims, slots, x_hbm, sx_hbm, sy_hbm, fx_hbm, fy_hbm, mid, load, sy_ref, fy_ref, sx_ref, fx_ref, xs, y_out, y_in, *rest):
     rows, cols, nx, ny = dims
     if slots:
         table, send, recv, y_table, y_send_buf, y_recv_buf, load_sem, x_send, x_recv, y_send, y_recv = rest
@@ -135,7 +141,7 @@
     ]
     small = [
         pltpu.make_async_copy(src, dst, load_sem.at[5 + k])
-        for k, (src, dst) in enumerate(((sx_hbm, sx_ref), (sy_hbm, sy_ref), (fx_hbm, fx_ref)))
+        for k, (src, dst) in enumerate(((sx_hbm, sx_ref), (fx_hbm, fx_ref), (sy_hbm, sy_ref), (fy_hbm, fy_ref)))
     ]
     for c in (*small, loads[0], loads[1], *y_loads, loads[2]):
         c.start()
@@ -217,6 +223,16 @@
     y_from, y_to = (y_send_buf, y_recv_buf) if slots else (y_out, y_in)
     y_copies = [remote(y_from.at[s], y_to.at[s], y_send.at[s], y_recv.at[s], (gx, (ym, yp)[s])) for s in range(2)]
 
+    def x_tiles(first, last, low, high, t0, t1):
+        def step(t, carry):
+            y = pl.multiple_of(t * 16, 16)
+            to = pl.multiple_of(lax.rem(t + 1, total // 16) * 16, 16)
+            x_tile(xs, mid, y, to, unit, wx, first, last, low, high)
+            return carry
+
+        lax.fori_loop(t0, t1, step, 0)
+
+    inner0, inner1 = TOP, rows - BOT
     loads[0].wait()
     if slots:
         pack(0, 0)
@@ -237,6 +253,7 @@
     for k in range(1, n):
         if k == n - 1:
             loads[2].wait()
+            x_tiles(inner0, inner1, TOP, TOP + rows - 1, 0, cols // 16)
             for s in range(2):
                 y_copies[s].wait_recv()
                 if slots:
@@ -247,20 +264,10 @@
                 pack(k, d)
             x_copies[k][d].start()
 
-    def x_tiles(first, last, low, high, t0, t1):
-        def step(t, carry):
-            y = pl.multiple_of(t * 16, 16)
-            to = pl.multiple_of(lax.rem(t + 1, total // 16) * 16, 16)
-            x_tile(xs, mid, y, to, unit, wx, first, last, low, high)
-            return carry
-
-        lax.fori_loop(t0, t1, step, 0)
-
     needs = [jnp.sum(need.astype(jnp.float32)) for ref in (sx_ref, sy_ref) for need in rows_needed(ref[...])]
     load[0] = functools.reduce(jnp.maximum, needs)
 
-    inner0, inner1 = TOP, rows - BOT
-    x_tiles(inner0, inner1, TOP, TOP + rows - 1, 0, total // 16)
+    x_tiles(inner0, inner1, TOP, TOP + rows - 1, cols // 16, total // 16)
 
     top = TOP + rows + BOT - 1
     for k in range(n):
@@ -301,13 +308,12 @@
     lax.fori_loop(0, rows, end, 0)
 
 
-def sweep_x(slots, collective_id, nx, ny, cells, sx, sy, fx):
+def sweep_x(slots, collective_id, nx, ny, cells, sx, sy, fx, fy):
     rows, cols, lanes = cells.shape
     n, total = CHUNKS, cols + 2 * PAD
     dma = pltpu.SemaphoreType.DMA
     bf16 = jnp.bfloat16
     scratch = [
-        pltpu.VMEM((1, lanes), jnp.int32),
         pltpu.VMEM((1, lanes), jnp.int32),
         pltpu.VMEM((1, lanes), jnp.float32),
         pltpu.VMEM((rows + TOP + BOT, total, lanes), bf16),
@@ -323,21 +329,23 @@
             pltpu.VMEM((2, slots, rows, lanes), bf16),
             pltpu.VMEM((2, slots, rows, lanes), bf16),
         ]
-    scratch += [dma((8,)), dma((2, n)), dma((2, n)), dma((2,)), dma((2,))]
+    scratch += [dma((9,)), dma((2, n)), dma((2, n)), dma((2,)), dma((2,))]
     vmem = pl.BlockSpec(memory_space=pltpu.VMEM)
     return pl.pallas_call(
         functools.partial(exchange, (rows, cols, nx, ny), slots),
         out_shape=(
             pltpu.VMEM((rows, total, lanes), jnp.float32),
             jax.ShapeDtypeStruct((1,), jnp.float32),
+            pltpu.VMEM((1, lanes), jnp.int32),
+            pltpu.VMEM((1, lanes), jnp.float32),
         ),
-        in_specs=[pl.BlockSpec(memory_space=pltpu.HBM)] * 4,
-        out_specs=(vmem, pl.BlockSpec(memory_space=pltpu.SMEM)),
+        in_specs=[pl.BlockSpec(memory_space=pltpu.HBM)] * 5,
+        out_specs=(vmem, pl.BlockSpec(memory_space=pltpu.SMEM), vmem, vmem),
         scratch_shapes=scratch,
         compiler_params=pltpu.CompilerParams(
             vmem_limit_bytes=52 * 1024 * 1024, collective_id=collective_id, has_side_effects=True
         ),
-    )(cells, sx, sy, fx)
+    )(cells, sx, sy, fx, fy)
 
 
 def sweep_y(mid, sy, fy):
@@ -361,12 +369,14 @@
 
 def body(nx, ny, cells, sx, sy, fx, fy):
     sx, sy, fx, fy = (a.reshape(1, LANES) for a in (sx, sy, fx, fy))
-    mid, load = sweep_x(SLOTS, 0, nx, ny, cells, sx, sy, fx)
-
-    out = sweep_y(mid, sy, fy)
+    args = (nx, ny, cells, sx, sy, fx, fy)
+    mid, load, *along_y = sweep_x(SLOTS, 0, *args)
+
+    out = sweep_y(mid, *along_y)
 
     def whole(out):
-        return sweep_y(sweep_x(0, 1, nx, ny, cells, sx, sy, fx)[0], sy, fy)
+        mid, _, *along_y = sweep_x(0, 1, *args)
+        return sweep_y(mid, *along_y)
 
     return lax.cond(load[0] <= SLOTS * LANES, lambda out: out, whole, out)
 

time: 32.3 us -> 29.3 us (0.907)
  the two profiles are of different devices: /device:TPU:0 before, /device:TPU:26 now
where the time goes in v3:
time: 29.3 us; the launch traced here: 29.2 us
  Pallas kernels  28.6 us (98%)
  between operations  0.63 us (2%)
    pallas_call x1, Pallas kernels, sweep_x(): pl.pallas_call(functools.partial(exchange, (rows, cols, nx, ny), slots),...  23.5 us
    pallas_call x1, Pallas kernels, sweep_y(): pl.pallas_call(functools.partial(finish, (rows, cols)), out_shape=pltpu.H...  5.06 us

profile of v3, /device:TPU:26, one launch (start us, length us, event | category | flops | bytes accessed | tf_op | source)
XLA Modules:
  0.0 29.2 jit_solution(8815944803800189625)
XLA Ops:
  0.0 23.5 %shard_map.57 = (f32[32,544,128]{2,1,0:T(8,128)S(1)}, f32[1]{0:T(128)}, s32[1,128]{1,0:T(1,128)S(1)}, f32[1,128]{1,0:T(1,128)S(1)}) custom-call(bf16[32,512,128]{2,1,0:T(8,128)(2,1)} %x_hbm.1, s32[1,128]{1,0:T(1,128)} %bitcast.5, s32[1,128]{1,0:T(1,128)} %bitcast.7, f32[1,128]{1,0:T(1,128)} %bitcast.9, f32[1,128]{1,0:T(1,128)} %bitcast.11), custom_call_target="tpu_custom_call" | custom-call | tf_op jit(solution)/shard_map/pallas_call | solution.py:334
  24.2 5.1 %shard_map.58 = f32[32,512,128]{2,1,0:T(8,128)} custom-call(f32[32,544,128]{2,1,0:T(8,128)S(1)} %get-tuple-element.32.mid, s32[1,128]{1,0:T(1,128)S(1)} %get-tuple-element.33.sy_ref, f32[1,128]{1,0:T(1,128)S(1)} %get-tuple-element.34.fy_ref), custom_call_target="tpu_custom_call" | custom-call | tf_op jit(solution)/shard_map/pallas_call | solution.py:356
  (1 shorter events, 0.0 us)
